TPU v7x, 256 devices: a whole 4x4x8 slice. The times are simulated.
256 devices in a mesh: rows: 32 (over y, x, core), outs: 8 (over z).
Axes of the slice: x: 4, y: 4, z: 8, core: 2. Of those that a mesh axis runs over, the one named last changes fastest.
Arguments:
- codes: int32 [49152, 256], P('rows'), may hold values from 0 to 31
- node_of_row: int32 [49152], P('rows'), may hold values from 0 to 15
- grad: bfloat16 [49152, 128], P('rows', 'outs'), may hold values from -6 to 6
- hess: bfloat16 [49152, 128], P('rows', 'outs'), may hold values from 0.099609375 to 1
- small_side: int32 [8], replicated, may hold values from 0 to 1
- evicted: int32 [8], replicated, may hold values from 0 to 1, as said below
- parent_hist: float32 [2, 8, 128, 8192], P(None, None, 'outs', 'rows'), as said below
Outputs:
- node_hist: float32 [2, 16, 128, 8192], P(None, None, 'outs', 'rows')
- split_gain: float32 [16, 8192], P(None, 'rows')
- best_gain: float32 [16], replicated
Inputs may be any that keep to these rules, and one draw needn't show every extreme that they name: `evicted`: exactly 3 of the 8 entries are 1. `parent_hist`: the hessian component is not negative.
All inputs are finite; a program needn't handle non-finite values.
Results may differ from a plain program's by a relative error of at most 0.0003.
Values may be sent and summed in bfloat16 or wider, within the bound.
A program may use at most 256 MiB of HBM per device.

v0:
```python
import jax
import jax.numpy as jnp
from jax import lax
from jax.sharding import PartitionSpec as P

BINS = 32
TARGETS = 128


def slot_values(grads, hesses, nodes, slots):
    count = grads.shape[0]
    hit = (nodes[:, None] == slots[None, :])[:, :, None]
    grad_part = jnp.where(hit, grads[:, None, :], jnp.zeros((), grads.dtype))
    hess_part = jnp.where(hit, hesses[:, None, :], jnp.zeros((), hesses.dtype))
    return jnp.concatenate([grad_part.reshape(count, -1), hess_part.reshape(count, -1)], axis=1)


def contract(block, values):
    count = block.shape[0]
    onehot = block[:, :, None] == jnp.arange(BINS, dtype=jnp.int32)[None, None, :]
    onehot = onehot.reshape(count, -1).astype(jnp.bfloat16)
    return lax.dot_general(
        onehot, values, (((0,), (0,)), ((), ())), preferred_element_type=jnp.float32
    )


def gain_terms(node_hist):
    grads = node_hist[0]
    hesses = node_hist[1]
    nodes, targets, span = grads.shape
    grads = grads.reshape(nodes, targets, span // BINS, BINS)
    hesses = hesses.reshape(nodes, targets, span // BINS, BINS)
    left_g = jnp.cumsum(grads, axis=3)
    left_h = jnp.cumsum(hesses, axis=3)
    total_g = left_g[..., -1:]
    total_h = left_h[..., -1:]

    def score(a, s):
        return a * a / (jnp.maximum(s, 0.0) + 1.0)

    gain = (
        score(left_g, left_h) + score(total_g - left_g, total_h - left_h) - score(total_g, total_h)
    )
    return jnp.sum(gain, axis=1).reshape(nodes, span)


def local(codes, node_of_row, grad, hess, small_side, evicted, parent_hist):
    pairs = small_side.shape[0]
    local_targets = grad.shape[1]
    slots = jnp.arange(2 * pairs, dtype=jnp.int32)
    slot_count = slots.shape[0]
    span = codes.shape[1] // lax.axis_size("rows") * BINS
    values = slot_values(grad, hess, node_of_row, slots)
    built = lax.psum_scatter(contract(codes, values), "rows", scatter_dimension=0, tiled=True)
    built = jnp.transpose(built.reshape(span, 2, slot_count, local_targets), (1, 2, 3, 0))
    small = (small_side == 0)[None, :, None, None]
    pair_view = built.reshape(2, pairs, 2, local_targets, span)
    child = jnp.where(small, pair_view[:, :, 0], pair_view[:, :, 1])
    rebuilt = jnp.where(small, pair_view[:, :, 1], pair_view[:, :, 0])
    gone = (evicted == 1)[None, :, None, None]
    sibling = jnp.where(gone, rebuilt, parent_hist - child)
    first = jnp.where(small, child, sibling)
    second = jnp.where(small, sibling, child)
    node_hist = jnp.stack([first, second], axis=2).reshape(2, 2 * pairs, local_targets, span)
    partial_gain = gain_terms(node_hist)
    split_gain = lax.psum(partial_gain, "outs") / TARGETS
    best_gain = lax.pmax(jnp.max(split_gain, axis=1), "rows")
    return (node_hist, split_gain, best_gain)


def solution(mesh):
    return jax.shard_map(
        local,
        mesh=mesh,
        in_specs=(
            P("rows", None),
            P("rows"),
            P("rows", "outs"),
            P("rows", "outs"),
            P(),
            P(),
            P(None, None, "outs", "rows"),
        ),
        out_specs=(P(None, None, "outs", "rows"), P(None, "rows"), P()),
        check_vma=False,
    )
```

profile of v0, /device:TPU:1, one launch (start us, length us, event | category | flops | bytes accessed | tf_op | source)
XLA Modules:
  0.0 378.4 jit_solution(12323342735052473486)
XLA Ops:
  7.2 0.0 reduce-scatter.2.cloned.1.call-start
  7.2 0.7 iota_compare_fusion
  7.9 3.0 copy.36
  11.0 0.1 eq.47
  11.1 11.0 %bitcast_compare_fusion = pred[1536,8192]{0,1:T(32,128)(4,1)S(1)} fusion(s32[8192]{0:T(1024)S(1)} %eq.47, s32[1536,256]{0,1:T(8,128)} %copy.36), kind=kLoop, calls=%fused_computation | loop fusion | flops 12582912 | bytes 14188544 | tf_op jit(solution)/shard_map/eq | solution.py:20
  22.1 1.3 broadcast_select_fusion.1
  23.4 18.1 %fusion = f32[8192,512]{1,0:T(8,128)} fusion(pred[1536,8192]{0,1:T(32,128)(4,1)S(1)} %bitcast_compare_fusion, bf16[1536,256]{0,1:T(8,128)(2,1)} %bitcast.57, bf16[1536,256]{0,1:T(8,128)(2,1)} %bitcast.56), kind=kOutput, calls=%fused_computation.1 | convolution fusion | flops 12888047616 | bytes 30932992 | tf_op jit(solution)/shard_map/dot_general | solution.py:22
  41.5 0.0 reduce-scatter.2.cloned.1.call-update
  41.5 0.6 copy-done.4
  42.2 125.0 %reduce-scatter.2.cloned.1.call-done = f32[256,512]{1,0:T(8,128)} async-done(((f32[8192,512]{1,0:T(8,128)}), f32[256,512]{1,0:T(8,128)}) %reduce-scatter.2.cloned.1.call-update) | async-done | bytes 524304 | tf_op jit(solution)/shard_map/reduce_scatter | solution.py:54
  167.1 1.2 copy.37
  168.4 0.1 select_bitcast_fusion.1
  168.6 0.6 copy-done
  169.3 0.3 reshape_squeeze.6
  169.5 47.2 %reduce_window_sum.17 = f32[16,16,8,32]{3,2,1,0:T(8,128)S(1)} reduce-window(f32[16,16,8,32]{3,2,1,0:T(8,128)S(1)} %reshape_squeeze.6, f32[]{:T(128)} %constant.10.clone.1), window={size=1x1x1x32 pad=0_0x0_0x0_0x31_0}, to_apply=%region_1.2 | reduce-window | flops 2031616 | bytes 524292 | tf_op jit(solution)/shard_map/jit(cumsum)/reduce_window_sum | solution.py:33
  216.7 0.3 slice.34
  217.0 1.4 copy.48
  218.5 1.6 copy.50
  220.1 0.3 reshape_squeeze.7
  220.4 47.2 %reduce_window_sum.18 = f32[16,16,8,32]{3,2,1,0:T(8,128)S(1)} reduce-window(f32[16,16,8,32]{3,2,1,0:T(8,128)S(1)} %reshape_squeeze.7, f32[]{:T(128)} %constant.10.clone.1), window={size=1x1x1x32 pad=0_0x0_0x0_0x31_0}, to_apply=%region_2.3 | reduce-window | flops 2031616 | bytes 524292 | tf_op jit(solution)/shard_map/jit(cumsum)/reduce_window_sum | solution.py:34
  267.5 0.3 slice.35
  267.9 1.4 copy.49
  269.3 2.2 copy.51
  271.5 1.0 pad_maximum_fusion
  272.5 0.9 divide_bitcast_fusion
  273.4 0.1 copy.46
  273.5 1.8 subtract_reduce_fusion
  275.3 0.1 reshape.64
  275.4 22.7 %psum.7 = f32[16,256]{1,0:T(8,128)S(1)} all-reduce(f32[16,256]{1,0:T(8,128)S(1)} %reshape.64), channel_id=1, replica_groups=mesh['rows'=32,'outs'=8] {'outs'}, use_global_device_ids=true, to_apply=%region_4.5 | all-reduce | flops 4096 | bytes 32768 | tf_op jit(solution)/shard_map/psum | solution.py:66
  298.1 0.7 fusion.8
  298.8 71.9 %pmax.7 = f32[16]{0:T(128)} all-reduce(f32[16]{0:T(128)S(1)} %get-tuple-element.3), channel_id=1, replica_groups=mesh['rows'=32,'outs'=8] {'rows'}, use_global_device_ids=true, to_apply=%region_6.7 | all-reduce | flops 16 | bytes 128 | tf_op jit(solution)/shard_map/pmax | solution.py:67
  370.7 0.8 copy.39
  (15 shorter events, 0.1 us)
Async XLA Ops:
  7.2 14.9 %copy-start.3 = (bf16[1536,16]{0,1:T(8,128)(2,1)S(1)}, bf16[1536,16]{0,1:T(8,128)(2,1)}, u32[]{:S(2)}) copy-start(bf16[1536,16]{0,1:T(8,128)(2,1)} %param.10) | copy-start | bytes 147460
  7.2 14.9 %copy-start.2 = (bf16[1536,16]{0,1:T(8,128)(2,1)S(1)}, bf16[1536,16]{0,1:T(8,128)(2,1)}, u32[]{:S(2)}) copy-start(bf16[1536,16]{0,1:T(8,128)(2,1)} %param.9) | copy-start | bytes 147460
  7.2 160.0 %reduce-scatter.2.cloned.1.call-start = ((), (), s32[]{:S(2)}) async-start(), calls=%async_computation.1 | async-start | bytes 17301504 | tf_op jit(solution)/shard_map/reduce_scatter | solution.py:54
  41.5 0.7 copy-start.4
  41.5 0.7 copy-start.5
  41.5 126.9 %copy-start.1 = (f32[2,8,16,256]{3,2,1,0:T(8,128)S(1)}, f32[2,8,16,256]{3,2,1,0:T(8,128)}, u32[]{:S(2)}) copy-start(f32[2,8,16,256]{3,2,1,0:T(8,128)} %param.13) | copy-start | bytes 786436
  168.5 0.7 copy-start
Sparse Core Ops, SparseCore 0:
  41.6 125.4 reduce-scatter.1
where the time goes:
time: 379 us; the launch traced here: 378 us
  waiting for transfers between devices  125 us (33%)
  other arithmetic  112 us (30%)
  blocking collectives  94.6 us (25%)
  matrix products  18.1 us (5%)
  local copies, waits for them, and re-layouts  14.6 us (4%)
  between operations  14.2 us (4%)
    reduce_scatter x1, waiting for transfers between devices, local(): lax.psum_scatter(contract(codes, values), 'rows', scatter_dimension=0, ti...  125 us
    pmax x1, blocking collectives, local(): best_gain = lax.pmax(jnp.max(split_gain, axis=1), 'rows')  71.9 us
    another operation x1, other arithmetic, gain_terms(): left_g = jnp.cumsum(grads, axis=3)  47.2 us
    another operation x1, other arithmetic, gain_terms(): left_h = jnp.cumsum(hesses, axis=3)  47.2 us
    psum x1, blocking collectives, local(): split_gain = lax.psum(partial_gain, 'outs') / TARGETS  22.7 us
    dot_general x1, matrix products, contract(): lax.dot_general(onehot, values, (((0,), (0,)), ((), ())), preferred_eleme...  18.1 us
    eq x1, other arithmetic, contract(): block[:, :, None] == jnp.arange(BINS, dtype=jnp.int32)[None, None, :]  11 us
  transfers between devices with their start and end apart: 1, of which 1 were waited for; matrix products, arithmetic and copies ran while one was open for 0% of the time, Pallas kernels for 0%

commit v1 on v0

--- a/solution.py
+++ b/solution.py
@@ -63,7 +63,7 @@
     second = jnp.where(small, sibling, child)
     node_hist = jnp.stack([first, second], axis=2).reshape(2, 2 * pairs, local_targets, span)
     partial_gain = gain_terms(node_hist)
-    split_gain = lax.psum(partial_gain, "outs") / TARGETS
+    split_gain = jnp.sum(lax.all_gather(partial_gain, "outs"), axis=0) / TARGETS
     best_gain = lax.pmax(jnp.max(split_gain, axis=1), "rows")
     return (node_hist, split_gain, best_gain)
 

time: 379 us -> 375 us (0.989)
  blocking collectives: 94.6 us -> 90.4 us
    psum x1 -> x0, blocking collectives: 22.7 us -> none  [local(): split_gain = lax.psum(partial_gain, 'outs') / TARGETS]
    all_gather x0 -> x1, blocking collectives: none -> 19.5 us  [local(): split_gain = jnp.sum(lax.all_gather(partial_gain, 'outs'), axis=0) / TARGETS]
where the time goes in v1:
time: 375 us; the launch traced here: 374 us
  waiting for transfers between devices  125 us (33%)
  other arithmetic  112 us (30%)
  blocking collectives  90.4 us (24%)
  matrix products  18.1 us (5%)
  local copies, waits for them, and re-layouts  14.6 us (4%)
  between operations  14.2 us (4%)
    reduce_scatter x1, waiting for transfers between devices, local(): lax.psum_scatter(contract(codes, values), 'rows', scatter_dimension=0, ti...  125 us
    pmax x1, blocking collectives, local(): best_gain = lax.pmax(jnp.max(split_gain, axis=1), 'rows')  70.9 us
    another operation x1, other arithmetic, gain_terms(): left_g = jnp.cumsum(grads, axis=3)  47.2 us
    another operation x1, other arithmetic, gain_terms(): left_h = jnp.cumsum(hesses, axis=3)  47.2 us
    all_gather x1, blocking collectives, local(): split_gain = jnp.sum(lax.all_gather(partial_gain, 'outs'), axis=0) / TARGETS  19.5 us
    dot_general x1, matrix products, contract(): lax.dot_general(onehot, values, (((0,), (0,)), ((), ())), preferred_eleme...  18.1 us
    eq x1, other arithmetic, contract(): block[:, :, None] == jnp.arange(BINS, dtype=jnp.int32)[None, None, :]  11 us
  transfers between devices with their start and end apart: 1, of which 1 were waited for; matrix products, arithmetic and copies ran while one was open for 0% of the time, Pallas kernels for 0%

profile of v1, /device:TPU:1, one launch (start us, length us, event | category | flops | bytes accessed | tf_op | source)
XLA Modules:
  0.0 374.3 jit_solution(9012721510448988134)
XLA Ops:
  7.2 0.0 reduce-scatter.2.cloned.1.call-start
  7.2 0.7 iota_compare_fusion
  7.9 3.0 copy.48
  11.0 0.1 eq.47
  11.1 11.0 %bitcast_compare_fusion = pred[1536,8192]{0,1:T(32,128)(4,1)S(1)} fusion(s32[8192]{0:T(1024)S(1)} %eq.47, s32[1536,256]{0,1:T(8,128)} %copy.48), kind=kLoop, calls=%fused_computation | loop fusion | flops 12582912 | bytes 14188544 | tf_op jit(solution)/shard_map/eq | solution.py:20
  22.1 1.3 broadcast_select_fusion.1
  23.4 18.1 %fusion = f32[8192,512]{1,0:T(8,128)} fusion(pred[1536,8192]{0,1:T(32,128)(4,1)S(1)} %bitcast_compare_fusion, bf16[1536,256]{0,1:T(8,128)(2,1)} %bitcast.57, bf16[1536,256]{0,1:T(8,128)(2,1)} %bitcast.56), kind=kOutput, calls=%fused_computation.1 | convolution fusion | flops 12888047616 | bytes 30932992 | tf_op jit(solution)/shard_map/dot_general | solution.py:22
  41.5 0.0 reduce-scatter.2.cloned.1.call-update
  41.5 0.6 copy-done.4
  42.2 125.0 %reduce-scatter.2.cloned.1.call-done = f32[256,512]{1,0:T(8,128)} async-done(((f32[8192,512]{1,0:T(8,128)}), f32[256,512]{1,0:T(8,128)}) %reduce-scatter.2.cloned.1.call-update) | async-done | bytes 524304 | tf_op jit(solution)/shard_map/reduce_scatter | solution.py:54
  167.1 1.2 copy.49
  168.4 0.1 select_bitcast_fusion.1
  168.6 0.6 copy-done
  169.3 0.3 reshape_squeeze.6
  169.5 47.2 %reduce_window_sum.17 = f32[16,16,8,32]{3,2,1,0:T(8,128)S(1)} reduce-window(f32[16,16,8,32]{3,2,1,0:T(8,128)S(1)} %reshape_squeeze.6, f32[]{:T(128)} %constant.10.clone.1), window={size=1x1x1x32 pad=0_0x0_0x0_0x31_0}, to_apply=%region_1.2 | reduce-window | flops 2031616 | bytes 524292 | tf_op jit(solution)/shard_map/jit(cumsum)/reduce_window_sum | solution.py:33
  216.7 0.3 slice.34
  217.0 1.4 copy.60
  218.5 1.6 copy.62
  220.1 0.3 reshape_squeeze.7
  220.4 47.2 %reduce_window_sum.18 = f32[16,16,8,32]{3,2,1,0:T(8,128)S(1)} reduce-window(f32[16,16,8,32]{3,2,1,0:T(8,128)S(1)} %reshape_squeeze.7, f32[]{:T(128)} %constant.10.clone.1), window={size=1x1x1x32 pad=0_0x0_0x0_0x31_0}, to_apply=%region_2.3 | reduce-window | flops 2031616 | bytes 524292 | tf_op jit(solution)/shard_map/jit(cumsum)/reduce_window_sum | solution.py:34
  267.5 0.3 slice.35
  267.9 1.4 copy.61
  269.3 2.2 copy.63
  271.5 1.0 pad_maximum_fusion
  272.5 0.9 divide_bitcast_fusion
  273.4 0.1 copy.58
  273.5 1.8 subtract_reduce_fusion
  275.3 0.1 all_gather_reshape.3
  275.4 19.5 %all_gather.3 = f32[8,16,256]{2,1,0:T(8,128)S(1)} all-gather(f32[1,16,256]{2,1,0:T(8,128)S(1)} %all_gather_reshape.3), channel_id=1, replica_groups=mesh['rows'=32,'outs'=8] {'outs'}, dimensions={0}, use_global_device_ids=true | all-gather | bytes 147456 | tf_op jit(solution)/shard_map/all_gather | solution.py:66
  294.9 0.7 fusion.8
  295.6 70.9 %pmax.7 = f32[16]{0:T(128)} all-reduce(f32[16]{0:T(128)S(1)} %get-tuple-element.3), channel_id=1, replica_groups=mesh['rows'=32,'outs'=8] {'rows'}, use_global_device_ids=true, to_apply=%region_6.7 | all-reduce | flops 16 | bytes 128 | tf_op jit(solution)/shard_map/pmax | solution.py:67
  366.6 0.8 copy.51
  (16 shorter events, 0.2 us)
Async XLA Ops:
  7.2 14.9 %copy-start.3 = (bf16[1536,16]{0,1:T(8,128)(2,1)S(1)}, bf16[1536,16]{0,1:T(8,128)(2,1)}, u32[]{:S(2)}) copy-start(bf16[1536,16]{0,1:T(8,128)(2,1)} %param.10) | copy-start | bytes 147460
  7.2 14.9 %copy-start.2 = (bf16[1536,16]{0,1:T(8,128)(2,1)S(1)}, bf16[1536,16]{0,1:T(8,128)(2,1)}, u32[]{:S(2)}) copy-start(bf16[1536,16]{0,1:T(8,128)(2,1)} %param.9) | copy-start | bytes 147460
  7.2 160.0 %reduce-scatter.2.cloned.1.call-start = ((), (), s32[]{:S(2)}) async-start(), calls=%async_computation.1 | async-start | bytes 17301504 | tf_op jit(solution)/shard_map/reduce_scatter | solution.py:54
  41.5 0.7 copy-start.4
  41.5 0.7 copy-start.5
  41.5 126.9 %copy-start.1 = (f32[2,8,16,256]{3,2,1,0:T(8,128)S(1)}, f32[2,8,16,256]{3,2,1,0:T(8,128)}, u32[]{:S(2)}) copy-start(f32[2,8,16,256]{3,2,1,0:T(8,128)} %param.13) | copy-start | bytes 786436
  168.5 0.7 copy-start
Sparse Core Ops, SparseCore 0:
  41.6 125.4 reduce-scatter.1
